TPU v7x, 32 devices: a whole 2x2x4 slice. The times are simulated.
32 devices in a mesh: dp: 16 (over z, y, core), head: 2 (over x).
Axes of the slice: x: 2, y: 2, z: 4, core: 2. Of those that a mesh axis runs over, the one named last changes fastest.
Arguments:
- inputs: bfloat16 [49152, 1024], P(('dp', 'head')), may hold values from -6 to 6
- time_embed: bfloat16 [16, 1024], P('dp'), may hold values from -6 to 6
- segment_ids: int32 [16, 3072], P('dp'), may hold values from 0 to 7, never falling along the last dimension, each value on 1 to 1536 neighbouring positions
- modulator_weight: bfloat16 [1024, 6144], P(None, 'head'), may hold values from -0.1875 to 0.1875
- modulator_bias: bfloat16 [6144], P('head'), may hold values from -3 to 3
- projection_weight: bfloat16 [1024, 3, 1024], P(None, None, 'head'), may hold values from -0.1875 to 0.1875
- projection_bias: bfloat16 [3, 1024], P(None, 'head'), may hold values from -3 to 3
- output_weight: bfloat16 [1024, 1024], P('head'), may hold values from -3 to 3
- output_bias: bfloat16 [1024], replicated, may hold values from -3 to 3
- expand_weight: bfloat16 [1024, 2048], P(None, 'head'), may hold values from -0.1875 to 0.1875
- expand_bias: bfloat16 [2048], P('head'), may hold values from -3 to 3
- contract_weight: bfloat16 [2048, 1024], P('head'), may hold values from -0.125 to 0.125
- contract_bias: bfloat16 [1024], replicated, may hold values from -3 to 3
- cotangent: bfloat16 [49152, 1024], P(('dp', 'head')), may hold values from -6 to 6
Outputs:
- layer_output: bfloat16 [49152, 1024], P(('dp', 'head'))
- grad_inputs: float32 [49152, 1024], P(('dp', 'head'))
- grad_embed: float32 [16, 1024], P('dp')
- grad_modulator_weight: float32 [1024, 6144], P(None, 'head')
- grad_modulator_bias: float32 [6144], P('head')
- grad_projection_weight: float32 [1024, 3, 1024], P(None, None, 'head')
- grad_projection_bias: float32 [3, 1024], P(None, 'head')
- grad_output_weight: float32 [1024, 1024], P('head')
- grad_output_bias: float32 [1024], replicated
- grad_expand_weight: float32 [1024, 2048], P(None, 'head')
- grad_expand_bias: float32 [2048], P('head')
- grad_contract_weight: float32 [2048, 1024], P('head')
- grad_contract_bias: float32 [1024], replicated
Inputs may be any that keep to these rules, and one draw needn't show every extreme that they name: `segment_ids`: in each row the ids never fall, each of the 8 utterances takes 1 to 1536 frames.
All inputs are finite; a program needn't handle non-finite values.
Results may differ from a plain program's by a relative error of at most 0.018.
Values may be sent and summed in bfloat16 or wider, within the bound.
A program may use at most 512 MiB of HBM per device.

v0:
```python
import jax
import jax.numpy as jnp
from jax import lax
from jax.sharding import PartitionSpec as P

HDIM = 64
ROW_LEN = 3072
precise_setting = lax.Precision.HIGHEST


def layer_norm(values):
    centre = values - jnp.mean(values, axis=-1, keepdims=True)
    spread = jnp.mean(centre * centre, axis=-1, keepdims=True)
    return centre * lax.rsqrt(spread + 1e-06)


def modulate(values, scale_part, shift_part):
    return layer_norm(values) * (1.0 + scale_part) + shift_part


def gelu_tanh(values):
    return jax.nn.gelu(values, approximate=True)


def rotate(values, cosine, sine):
    half = values.shape[-1] // 2
    turned = jnp.concatenate([-values[..., half:], values[..., :half]], axis=-1)
    return values * cosine + turned * sine


def rotate_back(grads, cosine, sine):
    half = grads.shape[-1] // 2
    scaled = grads * sine
    return grads * cosine + jnp.concatenate([scaled[..., half:], -scaled[..., :half]], axis=-1)


def rotary_tables(positions, width):
    half = width // 2
    freqs = 10000.0 ** (-jnp.arange(half, dtype=jnp.float32) * 2.0 / width)
    angles = positions.astype(jnp.float32)[:, None] * freqs[None, :]
    angles = jnp.concatenate([angles, angles], axis=-1)
    return (jnp.cos(angles)[:, None, :], jnp.sin(angles)[:, None, :])


def on_device(
    inputs,
    time_embed,
    segment_ids,
    modulator_weight,
    modulator_bias,
    projection_weight,
    projection_bias,
    output_weight,
    output_bias,
    expand_weight,
    expand_bias,
    contract_weight,
    contract_bias,
    cotangent,
):
    local_frames = inputs.shape[0]
    width = inputs.shape[1]
    head_index = lax.axis_index("head")
    rows_here = time_embed.shape[0]
    total = rows_here * ROW_LEN
    local_inner = projection_weight.shape[2]
    heads_here = local_inner // HDIM
    local_hidden = expand_weight.shape[1]
    local_mod = modulator_weight.shape[1]
    block = min(512, ROW_LEN)
    count_blocks = ROW_LEN // block
    factor = HDIM ** (-0.5)
    frames = inputs.astype(jnp.float32)
    place = head_index * local_frames + jnp.arange(local_frames, dtype=jnp.int32)
    owner = place // ROW_LEN
    member = (owner[:, None] == jnp.arange(rows_here, dtype=jnp.int32)[None, :]).astype(jnp.float32)
    embeds = time_embed.astype(jnp.float32)
    silu_low = jax.nn.silu(embeds).astype(jnp.bfloat16)
    own_mod = jnp.dot(
        silu_low, modulator_weight, preferred_element_type=jnp.float32
    ) + modulator_bias.astype(jnp.float32)
    modulation = lax.all_gather(own_mod, "head", axis=1, tiled=True)
    per_frame = jnp.dot(member, modulation, precision=precise_setting)
    shift_a, scale_a, gate_a, shift_f, scale_f, gate_f = jnp.split(per_frame, 6, axis=1)
    normed_a_full, pull_a = jax.vjp(modulate, frames, scale_a, shift_a)
    attention_normed = normed_a_full.astype(jnp.bfloat16)
    positions = jnp.arange(total, dtype=jnp.int32) % ROW_LEN
    cosine, sine = rotary_tables(positions, HDIM)
    weight_proj = projection_weight.reshape(width, 3 * local_inner)
    gathered_a = lax.all_gather(attention_normed, "head", axis=0, tiled=True)
    projected_rows = jnp.dot(gathered_a, weight_proj, preferred_element_type=jnp.float32)
    projected_rows = (projected_rows + projection_bias.astype(jnp.float32).reshape(-1)).reshape(
        total, 3, heads_here, HDIM
    )
    queries = rotate(projected_rows[:, 0], cosine, sine).astype(jnp.bfloat16)
    keys = rotate(projected_rows[:, 1], cosine, sine).astype(jnp.bfloat16)
    values = projected_rows[:, 2].astype(jnp.bfloat16)
    query_rows = queries.reshape(rows_here, ROW_LEN, heads_here, HDIM)
    key_rows = keys.reshape(rows_here, ROW_LEN, heads_here, HDIM)
    value_rows = values.reshape(rows_here, ROW_LEN, heads_here, HDIM)
    block_ids = jnp.arange(count_blocks, dtype=jnp.int32)

    def block_scores(query_block, key_row, segment_block, segment_row):
        scores = (
            jnp.einsum("qhd,khd->hqk", query_block, key_row, preferred_element_type=jnp.float32)
            * factor
        )
        allowed = (segment_block[:, None] == segment_row[None, :])[None]
        return jnp.where(allowed, scores, -1e30)

    def attend_row(operands):
        query_row, key_row, value_row, segment_row = operands

        def attend_block(carry, index):
            start = index * block
            query_block = lax.dynamic_slice_in_dim(query_row, start, block, 0)
            segment_block = lax.dynamic_slice_in_dim(segment_row, start, block, 0)
            scores = block_scores(query_block, key_row, segment_block, segment_row)
            peak = jnp.max(scores, axis=-1, keepdims=True)
            expo = jnp.exp(scores - peak)
            mass = jnp.sum(expo, axis=-1, keepdims=True)
            weights = (expo / mass).astype(jnp.bfloat16)
            result = jnp.einsum(
                "hqk,khd->qhd", weights, value_row, preferred_element_type=jnp.float32
            )
            return (carry, (result, (peak + jnp.log(mass))[..., 0]))

        _, (results, log_mass) = lax.scan(attend_block, jnp.zeros((), jnp.float32), block_ids)
        return (results.reshape(ROW_LEN, heads_here, HDIM), log_mass)

    attended_rows, log_mass_rows = lax.map(
        attend_row, (query_rows, key_rows, value_rows, segment_ids)
    )
    attended = attended_rows.reshape(total, local_inner).astype(jnp.bfloat16)
    part = attended
    branch_a = lax.psum_scatter(
        jnp.dot(part, output_weight, preferred_element_type=jnp.float32),
        "head",
        scatter_dimension=0,
        tiled=True,
    ) + output_bias.astype(jnp.float32)
    middle = frames + gate_a * branch_a
    normed_f_full, pull_f = jax.vjp(modulate, middle, scale_f, shift_f)
    normed_f = normed_f_full.astype(jnp.bfloat16)
    full_expand, full_expand_bias, full_contract = (
        lax.all_gather(expand_weight, "head", axis=1, tiled=True),
        lax.all_gather(expand_bias, "head", axis=0, tiled=True),
        lax.all_gather(contract_weight, "head", axis=0, tiled=True),
    )
    hidden_pre = jnp.dot(
        normed_f, full_expand, preferred_element_type=jnp.float32
    ) + full_expand_bias.astype(jnp.float32)
    hidden_full, gelu_pull = jax.vjp(gelu_tanh, hidden_pre)
    hidden = hidden_full.astype(jnp.bfloat16)
    branch_f = jnp.dot(
        hidden, full_contract, preferred_element_type=jnp.float32
    ) + contract_bias.astype(jnp.float32)
    result = middle + gate_f * branch_f
    layer_output = result.astype(jnp.bfloat16)
    grad_out = cotangent.astype(jnp.float32)
    grad_gate_f = grad_out * branch_f
    grad_branch_f = (gate_f * grad_out).astype(jnp.bfloat16)
    bias_down = jnp.sum(grad_branch_f.astype(jnp.float32), axis=0)
    grad_hidden = jnp.einsum(
        "fd,hd->fh", grad_branch_f, full_contract, preferred_element_type=jnp.float32
    )
    contract_part = jnp.einsum(
        "fh,fd->hd", hidden, grad_branch_f, preferred_element_type=jnp.float32
    )
    grad_pre = gelu_pull(grad_hidden)[0].astype(jnp.bfloat16)
    expand_part = jnp.einsum("fd,fh->dh", normed_f, grad_pre, preferred_element_type=jnp.float32)
    expand_bias_slice = jnp.sum(grad_pre.astype(jnp.float32), axis=0)
    grad_normed_f = jnp.einsum(
        "fh,dh->fd", grad_pre, full_expand, preferred_element_type=jnp.float32
    )
    grad_expand, grad_expand_bias, grad_contract = (
        lax.psum_scatter(
            expand_part.astype(jnp.bfloat16), "head", scatter_dimension=1, tiled=True
        ).astype(jnp.float32),
        lax.psum_scatter(
            expand_bias_slice.astype(jnp.bfloat16), "head", scatter_dimension=0, tiled=True
        ).astype(jnp.float32),
        lax.psum_scatter(
            contract_part.astype(jnp.bfloat16), "head", scatter_dimension=0, tiled=True
        ).astype(jnp.float32),
    )
    grad_middle_part, grad_scale_f, grad_shift_f = pull_f(grad_normed_f)
    grad_middle = grad_out + grad_middle_part
    grad_gate_a = grad_middle * branch_a
    grad_branch_a = (gate_a * grad_middle).astype(jnp.bfloat16)
    bias_out = jnp.sum(grad_branch_a.astype(jnp.float32), axis=0)
    grad_branch_rows = lax.all_gather(grad_branch_a, "head", axis=0, tiled=True)
    grad_attended = jnp.einsum(
        "fd,id->fi", grad_branch_rows, output_weight, preferred_element_type=jnp.float32
    ).astype(jnp.bfloat16)
    grad_output = jnp.einsum(
        "fi,fd->id", attended, grad_branch_rows, preferred_element_type=jnp.float32
    )
    grad_attended_rows = grad_attended.reshape(rows_here, ROW_LEN, heads_here, HDIM)

    def attend_back(operands):
        query_row, key_row, value_row, segment_row, grad_row, log_mass = operands

        def back_block(carry, step_inputs):
            key_total, value_total = carry
            index, mass_block = step_inputs
            start = index * block
            query_block = lax.dynamic_slice_in_dim(query_row, start, block, 0)
            segment_block = lax.dynamic_slice_in_dim(segment_row, start, block, 0)
            grad_block = lax.dynamic_slice_in_dim(grad_row, start, block, 0)
            scores = block_scores(query_block, key_row, segment_block, segment_row)
            probs = jnp.exp(scores - mass_block[:, :, None])
            grad_probs = jnp.einsum(
                "qhd,khd->hqk", grad_block, value_row, preferred_element_type=jnp.float32
            )
            centre = jnp.sum(grad_probs * probs, axis=-1, keepdims=True)
            grad_scores = (probs * (grad_probs - centre)).astype(jnp.bfloat16)
            grad_query = (
                jnp.einsum("hqk,khd->qhd", grad_scores, key_row, preferred_element_type=jnp.float32)
                * factor
            )
            key_total = (
                key_total
                + jnp.einsum(
                    "hqk,qhd->khd", grad_scores, query_block, preferred_element_type=jnp.float32
                )
                * factor
            )
            value_total = value_total + jnp.einsum(
                "hqk,qhd->khd",
                probs.astype(jnp.bfloat16),
                grad_block,
                preferred_element_type=jnp.float32,
            )
            return ((key_total, value_total), grad_query)

        empty = jnp.zeros((ROW_LEN, heads_here, HDIM), jnp.float32)
        (grad_key_row, grad_value_row), grad_query_blocks = lax.scan(
            back_block, (empty, empty), (block_ids, log_mass)
        )
        return (grad_query_blocks.reshape(ROW_LEN, heads_here, HDIM), grad_key_row, grad_value_row)

    grad_query_rows, grad_key_rows, grad_value_rows = lax.map(
        attend_back,
        (query_rows, key_rows, value_rows, segment_ids, grad_attended_rows, log_mass_rows),
    )
    grad_query_pre = rotate_back(grad_query_rows.reshape(total, heads_here, HDIM), cosine, sine)
    grad_key_pre = rotate_back(grad_key_rows.reshape(total, heads_here, HDIM), cosine, sine)
    grad_value_pre = grad_value_rows.reshape(total, heads_here, HDIM)
    grad_projected = jnp.stack([grad_query_pre, grad_key_pre, grad_value_pre], axis=1).astype(
        jnp.bfloat16
    )
    inner_start = head_index * local_inner
    grad_projected = grad_projected.reshape(total, 3 * local_inner)
    grad_projection = jnp.einsum(
        "fd,fc->dc", gathered_a, grad_projected, preferred_element_type=jnp.float32
    )
    grad_projection = grad_projection.reshape(width, 3, local_inner)
    grad_projection_bias = jnp.sum(grad_projected.astype(jnp.float32), axis=0).reshape(
        3, local_inner
    )
    part = grad_projected
    grad_normed_a = lax.psum_scatter(
        jnp.einsum("fc,dc->fd", part, weight_proj, preferred_element_type=jnp.float32).astype(
            jnp.bfloat16
        ),
        "head",
        scatter_dimension=0,
        tiled=True,
    ).astype(jnp.float32)
    full_proj_bias = lax.dynamic_update_slice(
        jnp.zeros((3, local_inner * lax.axis_size("head")), jnp.float32),
        grad_projection_bias,
        (jnp.int32(0), inner_start),
    )
    grad_frames_part, grad_scale_a, grad_shift_a = pull_a(grad_normed_a)
    grad_inputs = grad_middle + grad_frames_part
    grad_per_frame = jnp.concatenate(
        [grad_shift_a, grad_scale_a, grad_gate_a, grad_shift_f, grad_scale_f, grad_gate_f], axis=1
    )
    grad_per_row = jnp.dot(member.T, grad_per_frame, precision=precise_setting)
    grad_mod = lax.psum_scatter(grad_per_row, "head", scatter_dimension=1, tiled=True)
    grad_mod_weight = jnp.dot(silu_low.astype(jnp.float32).T, grad_mod, precision=precise_setting)
    grad_mod_bias = jnp.sum(grad_mod, axis=0)
    grad_silu_part = jnp.dot(
        grad_mod, modulator_weight.astype(jnp.float32).T, precision=precise_setting
    )
    grad_silu = lax.psum(grad_silu_part, "head")
    _, silu_pull = jax.vjp(jax.nn.silu, embeds)
    grad_embed = silu_pull(grad_silu)[0]
    grad_mod_weight, grad_projection, grad_output, grad_expand, grad_contract = (
        lax.psum(grad_mod_weight.astype(jnp.bfloat16), "dp").astype(jnp.float32),
        lax.psum(grad_projection.astype(jnp.bfloat16), "dp").astype(jnp.float32),
        lax.psum(grad_output.astype(jnp.bfloat16), "dp").astype(jnp.float32),
        lax.psum(grad_expand.astype(jnp.bfloat16), "dp").astype(jnp.float32),
        lax.psum(grad_contract.astype(jnp.bfloat16), "dp").astype(jnp.float32),
    )
    mod_start = head_index * local_mod
    hidden_start = head_index * local_hidden
    full_mod_bias = lax.dynamic_update_slice(
        jnp.zeros((local_mod * lax.axis_size("head"),), jnp.float32), grad_mod_bias, (mod_start,)
    )
    full_hidden_bias = lax.dynamic_update_slice(
        jnp.zeros((local_hidden * lax.axis_size("head"),), jnp.float32),
        grad_expand_bias,
        (hidden_start,),
    )
    full_mod_bias, full_proj_bias, full_hidden_bias, bias_out, bias_down = lax.psum(
        (full_mod_bias, full_proj_bias, full_hidden_bias, bias_out, bias_down), ("dp", "head")
    )
    grad_mod_bias = lax.dynamic_slice_in_dim(full_mod_bias, mod_start, local_mod, 0)
    grad_projection_bias = lax.dynamic_slice_in_dim(full_proj_bias, inner_start, local_inner, 1)
    grad_expand_bias = lax.dynamic_slice_in_dim(full_hidden_bias, hidden_start, local_hidden, 0)
    return (
        layer_output,
        grad_inputs,
        grad_embed,
        grad_mod_weight,
        grad_mod_bias,
        grad_projection,
        grad_projection_bias,
        grad_output,
        bias_out,
        grad_expand,
        grad_expand_bias,
        grad_contract,
        bias_down,
    )


def solution(mesh):
    in_specs = (
        P(("dp", "head"), None),
        P("dp", None),
        P("dp", None),
        P(None, "head"),
        P("head"),
        P(None, None, "head"),
        P(None, "head"),
        P("head", None),
        P(),
        P(None, "head"),
        P("head"),
        P("head", None),
        P(),
        P(("dp", "head"), None),
    )
    out_specs = (
        P(("dp", "head"), None),
        P(("dp", "head"), None),
        P("dp", None),
        P(None, "head"),
        P("head"),
        P(None, None, "head"),
        P(None, "head"),
        P("head", None),
        P(),
        P(None, "head"),
        P("head"),
        P("head", None),
        P(),
    )
    return jax.shard_map(
        on_device, mesh=mesh, in_specs=in_specs, out_specs=out_specs, check_vma=False
    )
```

profile of v0, /device:TPU:0, one launch (start us, length us, event | category | flops | bytes accessed | tf_op | source)
XLA Modules:
  0.0 2761.1 jit_solution(12866396884245281831)
XLA Ops:
  47.7 74.4 %all-gather.6.cloned.1.call-done = bf16[3072,1024]{1,0:T(8,128)(2,1)} async-done(((bf16[1536,1024]{1,0:T(8,128)(2,1)}), bf16[3072,1024]{1,0:T(8,128)(2,1)}) %all-gather.6.cloned.1.call-update) | async-done | bytes 6291472 | tf_op jit(solution)/shard_map/all_gather | solution.py:90
  175.7 402.5 %while.47 = (s32[]{:T(128)}, bf16[6,512,8,64]{1,3,2,0:T(8,128)(2,1)}, f32[6,8,512]{2,1,0:T(8,128)S(1)}, s32[6]{0:T(128)S(1)}, s32[3072]{0:T(1024)S(1)}, /*index=...) while((s32[]{:T(128)}, ...), condition=%wide.region_5.6_spmd, body=%wide.region_2.5_spmd.sunk | while | flops 3373789184 | bytes 177883360 | solution.py:128
  178.4 21.8 fusion.136
  200.2 22.0 fusion.137
  245.4 21.8 fusion.136
  267.2 22.0 fusion.137
  312.4 21.8 fusion.136
  334.2 22.0 fusion.137
  379.4 21.8 fusion.136
  401.2 22.0 fusion.137
  446.4 21.8 fusion.136
  468.2 22.0 fusion.137
  535.2 22.0 fusion.137
  598.1 138.9 %reduce-scatter.8.cloned.1.call-done = f32[1536,1024]{1,0:T(8,128)} async-done(((f32[3072,1024]{1,0:T(8,128)}), f32[1536,1024]{1,0:T(8,128)}) %reduce-scatter.8.cloned.1.call-update) | async-done | bytes 6291472 | tf_op jit(solution)/shard_map/reduce_scatter | solution.py:136
  759.6 35.7 %all-gather.8.cloned.1.call-done = bf16[1024,2048]{1,0:T(8,128)(2,1)} async-done(((bf16[1024,1024]{1,0:T(8,128)(2,1)}), bf16[1024,2048]{1,0:T(8,128)(2,1)}) %all-gather.8.cloned.1.call-update) | async-done | bytes 4194320 | tf_op jit(solution)/shard_map/all_gather | solution.py:146
  811.2 42.3 %all-gather.10.cloned.1.call-done = bf16[2048,1024]{1,0:T(8,128)(2,1)} async-done(((bf16[1024,1024]{1,0:T(8,128)(2,1)}), bf16[2048,1024]{1,0:T(8,128)(2,1)}) %all-gather.10.cloned.1.call-update) | async-done | bytes 4194320 | tf_op jit(solution)/shard_map/all_gather | solution.py:148
  919.0 80.4 %all-gather.12.cloned.1.call-done = bf16[3072,1024]{1,0:T(8,128)(2,1)} async-done(((bf16[1536,1024]{1,0:T(8,128)(2,1)}), bf16[3072,1024]{1,0:T(8,128)(2,1)}) %all-gather.12.cloned.1.call-update) | async-done | bytes 6291472 | tf_op jit(solution)/shard_map/all_gather | solution.py:192
  1007.0 1078.0 %while.48 = (s32[]{:T(128)}, f32[3072,8,64]{0,2,1:T(8,128)}, f32[3072,8,64]{0,2,1:T(8,128)}, f32[6,512,8,64]{1,0,3,2:T(8,128)}, s32[6]{0:T(128)S(1)}, /*index=5*...) while((s32[]{:T(128)}, f32[3072,8,64]{0,2,1:T(8,128)}, ...), condition=%wide.region_13.14_spmd.clone, body=%wide.region_11.13_spmd.clone.sunk | while | flops 8251502592 | bytes 425855200 | solution.py:238
  1030.4 23.5 bitcast_add_fusion.5
  1054.0 37.6 %multiply_reduce_fusion.4 = (f32[8,512]{1,0:T(8,128)S(1)}, f32[8,512,3072]{2,1,0:T(8,128)}) fusion(f32[8,512,3072]{2,1,0:T(8,128)} %fusion.148, f32[8,512]{1,0:T(8,128)S(1)} %dynamic-slice_bitcast_fusion.2, pred[512,3072]{1,0:T(8,128)(4,1)S(1)} %broadcast_compare_fusion.5, bf16[3072,8,64]{0,2,1:T(8,128)(2,1)} %get-tuple-element.509, ...), kind=kOutput, calls=%fused_computation.16.clone.1 | convolution fusion | flops 1673523200 | bytes 105938944 | tf_op jit(solution)/shard_map/while/body/eval_jaxpr/while/body/eval_jaxpr/qhd,khd->hqk/dot_general | solution.py:213
  1091.6 40.6 %multiply_convert_fusion.6 = bf16[8,512,3072]{2,1,0:T(8,128)(2,1)} fusion(f32[8,512,3072]{2,1,0:T(8,128)} %get-tuple-element.431, f32[8,512,3072]{2,1,0:T(8,128)} %fusion.148, f32[8,512]{1,0:T(8,128)S(1)} %get-tuple-element.432, f32[8,512]{1,0:T(8,128)S(1)} %dynamic-slice_bitcast_fusion.2, pred[512,3072]{1,0:T(8,128)(4,1)S(1)} %broadcast_compare_fusion.5), kind=kLoop, calls=%fused_computation.15.clone.1 | loop fusion | flops 75497472 | bytes 127434752 | tf_op jit(solution)/shard_map/while/body/eval_jaxpr/while/body/eval_jaxpr/convert_element_type | solution.py:217
  1162.3 21.8 dynamic_update_slice.45
  1207.3 25.0 bitcast_add_fusion.5
  1232.3 37.7 %multiply_reduce_fusion.4 = (f32[8,512]{1,0:T(8,128)S(1)}, f32[8,512,3072]{2,1,0:T(8,128)}) fusion(f32[8,512,3072]{2,1,0:T(8,128)} %fusion.148, f32[8,512]{1,0:T(8,128)S(1)} %dynamic-slice_bitcast_fusion.2, pred[512,3072]{1,0:T(8,128)(4,1)S(1)} %broadcast_compare_fusion.5, bf16[3072,8,64]{0,2,1:T(8,128)(2,1)} %get-tuple-element.509, ...), kind=kOutput, calls=%fused_computation.16.clone.1 | convolution fusion | flops 1673523200 | bytes 105938944 | tf_op jit(solution)/shard_map/while/body/eval_jaxpr/while/body/eval_jaxpr/qhd,khd->hqk/dot_general | solution.py:213
  1270.0 40.6 %multiply_convert_fusion.6 = bf16[8,512,3072]{2,1,0:T(8,128)(2,1)} fusion(f32[8,512,3072]{2,1,0:T(8,128)} %get-tuple-element.431, f32[8,512,3072]{2,1,0:T(8,128)} %fusion.148, f32[8,512]{1,0:T(8,128)S(1)} %get-tuple-element.432, f32[8,512]{1,0:T(8,128)S(1)} %dynamic-slice_bitcast_fusion.2, pred[512,3072]{1,0:T(8,128)(4,1)S(1)} %broadcast_compare_fusion.5), kind=kLoop, calls=%fused_computation.15.clone.1 | loop fusion | flops 75497472 | bytes 127434752 | tf_op jit(solution)/shard_map/while/body/eval_jaxpr/while/body/eval_jaxpr/convert_element_type | solution.py:217
  1342.5 21.8 dynamic_update_slice.45
  1387.5 24.9 bitcast_add_fusion.5
  1412.4 37.7 %multiply_reduce_fusion.4 = (f32[8,512]{1,0:T(8,128)S(1)}, f32[8,512,3072]{2,1,0:T(8,128)}) fusion(f32[8,512,3072]{2,1,0:T(8,128)} %fusion.148, f32[8,512]{1,0:T(8,128)S(1)} %dynamic-slice_bitcast_fusion.2, pred[512,3072]{1,0:T(8,128)(4,1)S(1)} %broadcast_compare_fusion.5, bf16[3072,8,64]{0,2,1:T(8,128)(2,1)} %get-tuple-element.509, ...), kind=kOutput, calls=%fused_computation.16.clone.1 | convolution fusion | flops 1673523200 | bytes 105938944 | tf_op jit(solution)/shard_map/while/body/eval_jaxpr/while/body/eval_jaxpr/qhd,khd->hqk/dot_general | solution.py:213
  1450.1 40.6 %multiply_convert_fusion.6 = bf16[8,512,3072]{2,1,0:T(8,128)(2,1)} fusion(f32[8,512,3072]{2,1,0:T(8,128)} %get-tuple-element.431, f32[8,512,3072]{2,1,0:T(8,128)} %fusion.148, f32[8,512]{1,0:T(8,128)S(1)} %get-tuple-element.432, f32[8,512]{1,0:T(8,128)S(1)} %dynamic-slice_bitcast_fusion.2, pred[512,3072]{1,0:T(8,128)(4,1)S(1)} %broadcast_compare_fusion.5), kind=kLoop, calls=%fused_computation.15.clone.1 | loop fusion | flops 75497472 | bytes 127434752 | tf_op jit(solution)/shard_map/while/body/eval_jaxpr/while/body/eval_jaxpr/convert_element_type | solution.py:217
  1522.6 21.8 dynamic_update_slice.45
  1567.6 24.9 bitcast_add_fusion.5
  1592.5 37.7 %multiply_reduce_fusion.4 = (f32[8,512]{1,0:T(8,128)S(1)}, f32[8,512,3072]{2,1,0:T(8,128)}) fusion(f32[8,512,3072]{2,1,0:T(8,128)} %fusion.148, f32[8,512]{1,0:T(8,128)S(1)} %dynamic-slice_bitcast_fusion.2, pred[512,3072]{1,0:T(8,128)(4,1)S(1)} %broadcast_compare_fusion.5, bf16[3072,8,64]{0,2,1:T(8,128)(2,1)} %get-tuple-element.509, ...), kind=kOutput, calls=%fused_computation.16.clone.1 | convolution fusion | flops 1673523200 | bytes 105938944 | tf_op jit(solution)/shard_map/while/body/eval_jaxpr/while/body/eval_jaxpr/qhd,khd->hqk/dot_general | solution.py:213
  1630.2 40.6 %multiply_convert_fusion.6 = bf16[8,512,3072]{2,1,0:T(8,128)(2,1)} fusion(f32[8,512,3072]{2,1,0:T(8,128)} %get-tuple-element.431, f32[8,512,3072]{2,1,0:T(8,128)} %fusion.148, f32[8,512]{1,0:T(8,128)S(1)} %get-tuple-element.432, f32[8,512]{1,0:T(8,128)S(1)} %dynamic-slice_bitcast_fusion.2, pred[512,3072]{1,0:T(8,128)(4,1)S(1)} %broadcast_compare_fusion.5), kind=kLoop, calls=%fused_computation.15.clone.1 | loop fusion | flops 75497472 | bytes 127434752 | tf_op jit(solution)/shard_map/while/body/eval_jaxpr/while/body/eval_jaxpr/convert_element_type | solution.py:217
  1702.6 21.8 dynamic_update_slice.45
  1747.7 24.9 bitcast_add_fusion.5
  1772.6 37.7 %multiply_reduce_fusion.4 = (f32[8,512]{1,0:T(8,128)S(1)}, f32[8,512,3072]{2,1,0:T(8,128)}) fusion(f32[8,512,3072]{2,1,0:T(8,128)} %fusion.148, f32[8,512]{1,0:T(8,128)S(1)} %dynamic-slice_bitcast_fusion.2, pred[512,3072]{1,0:T(8,128)(4,1)S(1)} %broadcast_compare_fusion.5, bf16[3072,8,64]{0,2,1:T(8,128)(2,1)} %get-tuple-element.509, ...), kind=kOutput, calls=%fused_computation.16.clone.1 | convolution fusion | flops 1673523200 | bytes 105938944 | tf_op jit(solution)/shard_map/while/body/eval_jaxpr/while/body/eval_jaxpr/qhd,khd->hqk/dot_general | solution.py:213
  1810.3 40.6 %multiply_convert_fusion.6 = bf16[8,512,3072]{2,1,0:T(8,128)(2,1)} fusion(f32[8,512,3072]{2,1,0:T(8,128)} %get-tuple-element.431, f32[8,512,3072]{2,1,0:T(8,128)} %fusion.148, f32[8,512]{1,0:T(8,128)S(1)} %get-tuple-element.432, f32[8,512]{1,0:T(8,128)S(1)} %dynamic-slice_bitcast_fusion.2, pred[512,3072]{1,0:T(8,128)(4,1)S(1)} %broadcast_compare_fusion.5), kind=kLoop, calls=%fused_computation.15.clone.1 | loop fusion | flops 75497472 | bytes 127434752 | tf_op jit(solution)/shard_map/while/body/eval_jaxpr/while/body/eval_jaxpr/convert_element_type | solution.py:217
  1882.7 21.8 dynamic_update_slice.45
  1927.8 24.9 bitcast_add_fusion.5
  1952.7 37.6 %multiply_reduce_fusion.4 = (f32[8,512]{1,0:T(8,128)S(1)}, f32[8,512,3072]{2,1,0:T(8,128)}) fusion(f32[8,512,3072]{2,1,0:T(8,128)} %fusion.148, f32[8,512]{1,0:T(8,128)S(1)} %dynamic-slice_bitcast_fusion.2, pred[512,3072]{1,0:T(8,128)(4,1)S(1)} %broadcast_compare_fusion.5, bf16[3072,8,64]{0,2,1:T(8,128)(2,1)} %get-tuple-element.509, ...), kind=kOutput, calls=%fused_computation.16.clone.1 | convolution fusion | flops 1673523200 | bytes 105938944 | tf_op jit(solution)/shard_map/while/body/eval_jaxpr/while/body/eval_jaxpr/qhd,khd->hqk/dot_general | solution.py:213
  1990.3 40.6 %multiply_convert_fusion.6 = bf16[8,512,3072]{2,1,0:T(8,128)(2,1)} fusion(f32[8,512,3072]{2,1,0:T(8,128)} %get-tuple-element.431, f32[8,512,3072]{2,1,0:T(8,128)} %fusion.148, f32[8,512]{1,0:T(8,128)S(1)} %get-tuple-element.432, f32[8,512]{1,0:T(8,128)S(1)} %dynamic-slice_bitcast_fusion.2, pred[512,3072]{1,0:T(8,128)(4,1)S(1)} %broadcast_compare_fusion.5), kind=kLoop, calls=%fused_computation.15.clone.1 | loop fusion | flops 75497472 | bytes 127434752 | tf_op jit(solution)/shard_map/while/body/eval_jaxpr/while/body/eval_jaxpr/convert_element_type | solution.py:217
  2062.8 21.8 dynamic_update_slice.45
  2146.5 77.2 %reduce-scatter.10.cloned.1.call-done = bf16[1536,1024]{1,0:T(8,128)(2,1)} async-done(((bf16[3072,1024]{1,0:T(8,128)(2,1)}), bf16[1536,1024]{1,0:T(8,128)(2,1)}) %reduce-scatter.10.cloned.1.call-update) | async-done | bytes 3145744 | tf_op jit(solution)/shard_map/reduce_scatter | solution.py:263
  2269.2 35.1 %convolution_bitcast_fusion = f32[6144,1]{1,0:T(8,128)} fusion(pred[1536,1]{0,1:T(4,128)(4,1)S(1)} %reshape.351, f32[1536,6144]{1,0:T(8,128)} %fusion.46), kind=kOutput, calls=%fused_computation.69 | convolution fusion | flops 113246208 | bytes 37774848
  2354.9 50.2 %reduce-scatter.12.cloned.1.call-done = bf16[1024,1024]{1,0:T(8,128)(2,1)} async-done(((bf16[1024,2048]{1,0:T(8,128)(2,1)}), bf16[1024,1024]{1,0:T(8,128)(2,1)}) %reduce-scatter.12.cloned.1.call-update) | async-done | bytes 2097168 | tf_op jit(solution)/shard_map/reduce_scatter | solution.py:177
  2405.1 57.3 %reduce-scatter.14.cloned.1.call-done = bf16[1024,1024]{1,0:T(8,128)(2,1)} async-done(((bf16[2048,1024]{1,0:T(8,128)(2,1)}), bf16[1024,1024]{1,0:T(8,128)(2,1)}) %reduce-scatter.14.cloned.1.call-update) | async-done | bytes 2097168 | tf_op jit(solution)/shard_map/reduce_scatter | solution.py:183
  2469.7 42.2 %all-reduce.1 = (f32[6144]{0:T(1024)S(1)}, f32[3,1024]{1,0:T(4,128)S(1)}, f32[1024]{0:T(1024)}, f32[2048]{0:T(1024)S(1)}, f32[1024]{0:T(1024)}) all-reduce(f32[6144]{0:T(1024)S(1)} %dynamic_update_slice.32, f32[3,1024]{1,0:T(4,128)S(1)} %constant_dynamic-update-slice_fusion.1, ...), channel_id=1, replica_groups=mesh['dp'=16,'head'=2] {'dp','head'}, use_global_device_ids=true, to_apply=%region_20.21 | all-reduce | flops 13312 | bytes 106496 | tf_op jit(solution)/shard_map/psum | solution.py:308
  2526.7 207.5 %all-reduce.5.cloned.1.call-done = (bf16[1024,3072]{1,0:T(8,128)(2,1)}, bf16[1024,3,512]{2,0,1:T(8,128)(2,1)}, bf16[512,1024]{1,0:T(8,128)(2,1)}, bf16[1024,1024]{1,0:T(8,128)(2,1)}, bf16[1024,1024]{1,0:T(8,128)(2,1)}) async-done(((bf16[1024,3072]{1,0:T(8,128)(2,1)}, bf16[1024,3,512]{2,0,1:T(8,128)(2,1)}, bf16[512,1024]{1,0:T(8,128)(2,1)}, bf16[1024,1024]{1,0:T(8,128)(2,1)}, bf16[1024,1024]{1,0:T(8,128)(2,1)}), ...) | async-done | bytes 14680080 | tf_op jit(solution)/shard_map/psum | solution.py:292
  (351 shorter events, 905.0 us)
Async XLA Ops:
  7.2 578.4 %copy-start = (bf16[512,1024]{1,0:T(8,128)(2,1)S(1)}, bf16[512,1024]{1,0:T(8,128)(2,1)}, u32[]{:S(2)}) copy-start(bf16[512,1024]{1,0:T(8,128)(2,1)} %param.25) | copy-start | bytes 3145732
  7.2 115.0 %all-gather.6.cloned.1.call-start = ((), (), s32[]{:S(2)}) async-start(), calls=%async_computation.5 | async-start | bytes 9437184 | tf_op jit(solution)/shard_map/all_gather | solution.py:90
  11.2 22.0 copy-start.23
  14.3 18.9 copy-start.27
  20.6 12.6 copy-start.3
  39.9 697.1 %reduce-scatter.8.cloned.1.call-start = ((), (), s32[]{:S(2)}) async-start(), calls=%async_computation.6 | async-start | bytes 18874368 | tf_op jit(solution)/shard_map/reduce_scatter | solution.py:136
  47.7 116.1 %copy-start.12 = (f32[3072,64]{0,1:T(8,128)}, f32[3072,64]{0,1:T(8,128)S(1)}, u32[]{:S(2)}) copy-start(f32[3072,64]{0,1:T(8,128)S(1)} %get-tuple-element.300) | copy-start | bytes 2359300
  47.7 116.1 %copy-start.15 = (f32[3072,64]{0,1:T(8,128)}, f32[3072,64]{0,1:T(8,128)S(1)}, u32[]{:S(2)}) copy-start(f32[3072,64]{0,1:T(8,128)S(1)} %get-tuple-element.301) | copy-start | bytes 2359300
  163.8 11.9 copy-start.22
  200.2 22.0 copy-start.2
  267.2 22.0 copy-start.2
  334.2 22.0 copy-start.2
  401.2 22.0 copy-start.2
  468.2 22.0 copy-start.2
  535.1 22.0 copy-start.2
  592.3 203.0 %all-gather.8.cloned.1.call-start = ((), (), s32[]{:S(2)}) async-start(), calls=%async_computation.7 | async-start | bytes 6291456 | tf_op jit(solution)/shard_map/all_gather | solution.py:146
  593.0 260.4 %all-gather.10.cloned.1.call-start = ((), (), s32[]{:S(2)}) async-start(), calls=%async_computation.8 | async-start | bytes 6291456 | tf_op jit(solution)/shard_map/all_gather | solution.py:148
  593.6 405.8 %all-gather.12.cloned.1.call-start = ((), (), s32[]{:S(2)}) async-start(), calls=%async_computation.9 | async-start | bytes 9437184 | tf_op jit(solution)/shard_map/all_gather | solution.py:192
  593.7 149.9 %copy-start.39 = (f32[1024]{0:T(1024)}, f32[1024]{0:T(1024)S(1)}, u32[]{:S(2)}) copy-start(f32[1024]{0:T(1024)S(1)} %convert_element_type.167) | copy-start | bytes 12292
  593.7 295.1 %copy-start.43 = (f32[1024]{0:T(1024)}, f32[1024]{0:T(1024)S(1)}, u32[]{:S(2)}) copy-start(f32[1024]{0:T(1024)S(1)} %convert_element_type.171) | copy-start | bytes 12292
  743.7 145.1 %copy-start.25 = (f32[1536]{0:T(1024)}, f32[1536]{0:T(1024)S(1)}, u32[]{:S(2)}) copy-start(f32[1536]{0:T(1024)S(1)} %broadcast_multiply_fusion.4) | copy-start | bytes 18436
  748.0 140.8 %copy-start.31 = (f32[1536]{0:T(1024)}, f32[1536]{0:T(1024)S(1)}, u32[]{:S(2)}) copy-start(f32[1536]{0:T(1024)S(1)} %fusion.67) | copy-start | bytes 18436
  795.3 79.9 %slice-start.2 = ((s8[6291456]{0:T(1024)(128)(4,1)}), s8[2097152]{0:T(1024)(128)(4,1)S(1)}, s32[]{:S(2)}) async-start(s8[6291456]{0:T(1024)(128)(4,1)} %bitcast.141), calls=%async_computation.17 | async-start | bytes 4194304
  853.5 21.8 slice-start.3
  853.5 21.8 copy-start.52
  910.3 8.6 copy-start.33
  918.9 1304.8 %reduce-scatter.10.cloned.1.call-start = ((), (), s32[]{:S(2)}) async-start(), calls=%async_computation.10 | async-start | bytes 9437184 | tf_op jit(solution)/shard_map/reduce_scatter | solution.py:263
  2094.3 9.4 copy-start.16
  2146.4 77.3 %copy-start.24 = (f32[1536]{0:T(1024)S(1)}, f32[1536]{0:T(1024)}, u32[]{:S(2)}) copy-start(f32[1536]{0:T(1024)} %copy-done.23) | copy-start | bytes 18436
  2146.4 202.5 %reduce-scatter.16.cloned.1.call-start = ((), (), s32[]{:S(2)}) async-start(), calls=%async_computation.13 | async-start | bytes 4718592 | tf_op jit(solution)/shard_map/reshape.47
  2146.5 83.8 %copy-start.30 = (f32[1536]{0:T(1024)S(1)}, f32[1536]{0:T(1024)}, u32[]{:S(2)}) copy-start(f32[1536]{0:T(1024)} %copy-done.29) | copy-start | bytes 18436
  2233.9 9.5 copy-start.7
  2233.9 9.5 copy-start.34
  2233.9 9.5 copy-start.40
  2233.9 21.5 slice-start.8
  2233.9 24.8 slice-start.4
  2243.4 12.0 slice-start.9
  2243.4 15.3 slice-start.5
  2304.3 100.9 %reduce-scatter.12.cloned.1.call-start = ((), (), s32[]{:S(2)}) async-start(), calls=%async_computation.11 | async-start | bytes 6291456 | tf_op jit(solution)/shard_map/reduce_scatter | solution.py:177
  2315.7 11.3 copy-start.45
  2315.7 146.7 %reduce-scatter.14.cloned.1.call-start = ((), (), s32[]{:S(2)}) async-start(), calls=%async_computation.12 | async-start | bytes 6291456 | tf_op jit(solution)/shard_map/reduce_scatter | solution.py:183
  2327.0 8.4 slice-start.10
  2327.0 407.2 %all-reduce.5.cloned.1.call-start = ((), (), s32[]{:S(2)}) async-start(), calls=%async_computation.14 | async-start | bytes 29360128 | tf_op jit(solution)/shard_map/psum | solution.py:292
  2462.4 50.8 %copy-start.17 = (f32[3072,1]{1,0:T(8,128)S(1)}, f32[3072,1]{1,0:T(8,128)}, u32[]{:S(2)}) copy-start(f32[3072,1]{1,0:T(8,128)} %reduce-scatter.16.cloned.1.call-done) | copy-start | bytes 36868
  2462.5 63.6 %copy-start.36 = (bf16[1,1024]{1,0:T(2,128)(2,1)S(1)}, bf16[1,1024]{1,0:T(2,128)(2,1)}, u32[]{:S(2)}) copy-start(bf16[1,1024]{1,0:T(2,128)(2,1)} %param.19) | copy-start | bytes 6148
  2462.5 63.6 %copy-start.38 = (f32[1,1024]{1,0:T(1,128)S(1)}, f32[1,1024]{1,0:T(1,128)}, u32[]{:S(2)}) copy-start(f32[1,1024]{1,0:T(1,128)} %copy-done.37) | copy-start | bytes 12292
  2734.2 9.6 slice-start.13
  2743.8 10.1 copy-start.1
  (36 other events, 164.3 us)
Sparse Core Ops, SparseCore 0:
  40.0 82.1 all-gather.5
  592.4 144.5 reduce-scatter.7
  738.5 56.7 all-gather.7
  796.7 56.7 all-gather.9
  919.0 80.3 all-gather.11
  2146.5 77.1 reduce-scatter.9
  2304.4 43.4 reduce-scatter.15
  2350.7 54.3 reduce-scatter.11
  2408.0 54.3 reduce-scatter.13
  2467.8 266.3 all-reduce.4
where the time goes:
time: 2770 us; the launch traced here: 2760 us
  matrix products  1140 us (41%)
  waiting for transfers between devices  765 us (28%)
  other arithmetic  554 us (20%)
  local copies, waits for them, and re-layouts  215 us (8%)
  blocking collectives  62 us (2%)
    dot_general x12, matrix products, block_scores(): jnp.einsum('qhd,khd->hqk', query_block, key_row, preferred_element_type=j...  257 us
    convert_element_type x6, other arithmetic, back_block(): grad_scores = (probs * (grad_probs - centre)).astype(jnp.bfloat16)  244 us
    dot_general x6, matrix products, back_block(): jnp.einsum('qhd,khd->hqk', grad_block, value_row, preferred_element_type=...  226 us
    psum x1, waiting for transfers between devices, on_device(): lax.psum(grad_mod_weight.astype(jnp.bfloat16), 'dp').astype(jnp.float32)  208 us
    dot_general x6, matrix products, back_block(): jnp.einsum('hqk,qhd->khd', probs.astype(jnp.bfloat16), grad_block, prefer...  148 us
    reduce_scatter x1, waiting for transfers between devices, on_device(): lax.psum_scatter(jnp.dot(part, output_weight, preferred_element_type=jnp....  139 us
    dynamic_update_slice x12, local copies, waits for them, and re-layouts, attend_row(): lax.scan(attend_block, jnp.zeros((), jnp.float32), block_ids)  137 us
    reduce_sum x6, other arithmetic, attend_block(): mass = jnp.sum(expo, axis=-1, keepdims=True)  132 us
  transfers between devices with their start and end apart: 10, of which 9 were waited for; matrix products, arithmetic and copies ran while one was open for 4% of the time, Pallas kernels for 0%

commit v1 on v0

--- a/solution.py
+++ b/solution.py
@@ -289,7 +289,9 @@
     _, silu_pull = jax.vjp(jax.nn.silu, embeds)
     grad_embed = silu_pull(grad_silu)[0]
     grad_mod_weight, grad_projection, grad_output, grad_expand, grad_contract = (
-        lax.psum(grad_mod_weight.astype(jnp.bfloat16), "dp").astype(jnp.float32),
+        jnp.sum(lax.all_gather(grad_mod_weight.astype(jnp.bfloat16), "dp"), axis=0).astype(
+            jnp.float32
+        ),
         lax.psum(grad_projection.astype(jnp.bfloat16), "dp").astype(jnp.float32),
         lax.psum(grad_output.astype(jnp.bfloat16), "dp").astype(jnp.float32),
         lax.psum(grad_expand.astype(jnp.bfloat16), "dp").astype(jnp.float32),

time: 2770 us -> 3100 us (1.12)
  waiting for transfers between devices: 765 us -> 1060 us
  other arithmetic: 554 us -> 594 us
    all_gather x0 -> x1, waiting for transfers between devices: none -> 414 us  [on_device(): lax.all_gather(grad_mod_weight.astype(jnp.bfloat16), 'dp')]
    reduce_scatter x1, waiting for transfers between devices: 50.2 us -> 0.01 us  [on_device(): lax.psum_scatter(expand_part.astype(jnp.bfloat16), 'head', scatter_dimens...]
    another operation x1, waiting for transfers between devices: 0.01 us -> 46.2 us
    psum x1, waiting for transfers between devices: 208 us -> 162 us  [on_device(): lax.psum(grad_projection.astype(jnp.bfloat16), 'dp').astype(jnp.float32)]
    reduce_scatter x1, waiting for transfers between devices: 77.2 us -> 38.6 us  [on_device(): lax.psum_scatter(jnp.einsum('fc,dc->fd', part, weight_proj, preferred_ele...]
    reduce_sum x0 -> x1, other arithmetic: none -> 34.8 us  [on_device(): jnp.sum(lax.all_gather(grad_mod_weight.astype(jnp.bfloat16), 'dp'), axis=0)]
    reduce_scatter x1, waiting for transfers between devices: 57.3 us -> 24.4 us  [on_device(): lax.psum_scatter(contract_part.astype(jnp.bfloat16), 'head', scatter_dime...]
  transfers between devices with their start and end apart: 10 -> 11, of which waited for: 9 -> 10; matrix products, arithmetic and copies ran while one was open for 4% -> 7% of each run, Pallas kernels for 0% -> 0%
where the time goes in v1:
time: 3100 us
  matrix products  1140 us (37%)
  waiting for transfers between devices  1060 us (34%)
  other arithmetic  594 us (19%)
  local copies, waits for them, and re-layouts  214 us (7%)
  blocking collectives  63.6 us (2%)
    all_gather x1, waiting for transfers between devices, on_device(): lax.all_gather(grad_mod_weight.astype(jnp.bfloat16), 'dp')  414 us
    dot_general x12, matrix products, block_scores(): jnp.einsum('qhd,khd->hqk', query_block, key_row, preferred_element_type=j...  256 us
    convert_element_type x6, other arithmetic, back_block(): grad_scores = (probs * (grad_probs - centre)).astype(jnp.bfloat16)  243 us
    dot_general x6, matrix products, back_block(): jnp.einsum('qhd,khd->hqk', grad_block, value_row, preferred_element_type=...  225 us
    psum x1, waiting for transfers between devices, on_device(): lax.psum(grad_projection.astype(jnp.bfloat16), 'dp').astype(jnp.float32)  162 us
    dot_general x6, matrix products, back_block(): jnp.einsum('hqk,qhd->khd', probs.astype(jnp.bfloat16), grad_block, prefer...  148 us
    reduce_scatter x1, waiting for transfers between devices, on_device(): lax.psum_scatter(jnp.dot(part, output_weight, preferred_element_type=jnp....  139 us
    dynamic_update_slice x12, local copies, waits for them, and re-layouts, attend_row(): lax.scan(attend_block, jnp.zeros((), jnp.float32), block_ids)  137 us
  transfers between devices with their start and end apart: 11, of which 10 were waited for; matrix products, arithmetic and copies ran while one was open for 7% of the time, Pallas kernels for 0%

profile of v1, /device:TPU:0, one launch (start us, length us, event | category | flops | bytes accessed | tf_op | source)
XLA Modules:
  0.0 3095.5 jit_solution(17761080375544014095)
XLA Ops:
  47.7 74.4 %all-gather.8.cloned.1.call-done = bf16[3072,1024]{1,0:T(8,128)(2,1)} async-done(((bf16[1536,1024]{1,0:T(8,128)(2,1)}), bf16[3072,1024]{1,0:T(8,128)(2,1)}) %all-gather.8.cloned.1.call-update) | async-done | bytes 6291472 | tf_op jit(solution)/shard_map/all_gather | solution.py:90
  175.7 402.1 %while.47 = (s32[]{:T(128)}, bf16[6,512,8,64]{1,3,2,0:T(8,128)(2,1)}, f32[6,8,512]{2,1,0:T(8,128)S(1)}, s32[6]{0:T(128)S(1)}, s32[3072]{0:T(1024)S(1)}, /*index=...) while((s32[]{:T(128)}, ...), condition=%wide.region_5.6_spmd, body=%wide.region_2.5_spmd.sunk | while | flops 3373789184 | bytes 177883360 | solution.py:128
  178.4 21.8 fusion.136
  200.2 22.0 fusion.137
  245.3 21.8 fusion.136
  267.1 22.0 fusion.137
  334.0 22.0 fusion.137
  400.9 22.0 fusion.137
  467.8 22.0 fusion.137
  534.7 22.0 fusion.137
  597.7 138.9 %reduce-scatter.8.cloned.1.call-done = f32[1536,1024]{1,0:T(8,128)} async-done(((f32[3072,1024]{1,0:T(8,128)}), f32[1536,1024]{1,0:T(8,128)}) %reduce-scatter.8.cloned.1.call-update) | async-done | bytes 6291472 | tf_op jit(solution)/shard_map/reduce_scatter | solution.py:136
  759.1 35.7 %all-gather.10.cloned.1.call-done = bf16[1024,2048]{1,0:T(8,128)(2,1)} async-done(((bf16[1024,1024]{1,0:T(8,128)(2,1)}), bf16[1024,2048]{1,0:T(8,128)(2,1)}) %all-gather.10.cloned.1.call-update) | async-done | bytes 4194320 | tf_op jit(solution)/shard_map/all_gather | solution.py:146
  810.8 42.3 %all-gather.12.cloned.1.call-done = bf16[2048,1024]{1,0:T(8,128)(2,1)} async-done(((bf16[1024,1024]{1,0:T(8,128)(2,1)}), bf16[2048,1024]{1,0:T(8,128)(2,1)}) %all-gather.12.cloned.1.call-update) | async-done | bytes 4194320 | tf_op jit(solution)/shard_map/all_gather | solution.py:148
  853.0 21.8 fusion.75
  918.6 80.4 %all-gather.14.cloned.1.call-done = bf16[3072,1024]{1,0:T(8,128)(2,1)} async-done(((bf16[1536,1024]{1,0:T(8,128)(2,1)}), bf16[3072,1024]{1,0:T(8,128)(2,1)}) %all-gather.14.cloned.1.call-update) | async-done | bytes 6291472 | tf_op jit(solution)/shard_map/all_gather | solution.py:192
  1006.6 1076.3 %while.48 = (s32[]{:T(128)}, f32[3072,8,64]{0,2,1:T(8,128)}, f32[3072,8,64]{0,2,1:T(8,128)}, f32[6,512,8,64]{1,0,3,2:T(8,128)}, s32[6]{0:T(128)S(1)}, /*index=5*...) while((s32[]{:T(128)}, f32[3072,8,64]{0,2,1:T(8,128)}, ...), condition=%wide.region_13.14_spmd.clone, body=%wide.region_11.13_spmd.clone.sunk | while | flops 8251502592 | bytes 425855200 | solution.py:238
  1030.0 23.6 bitcast_add_fusion.5
  1053.6 37.6 %multiply_reduce_fusion.4 = (f32[8,512]{1,0:T(8,128)S(1)}, f32[8,512,3072]{2,1,0:T(8,128)}) fusion(f32[8,512,3072]{2,1,0:T(8,128)} %fusion.148, f32[8,512]{1,0:T(8,128)S(1)} %dynamic-slice_bitcast_fusion.2, pred[512,3072]{1,0:T(8,128)(4,1)S(1)} %broadcast_compare_fusion.5, bf16[3072,8,64]{0,2,1:T(8,128)(2,1)} %get-tuple-element.508, ...), kind=kOutput, calls=%fused_computation.16.clone.1 | convolution fusion | flops 1673523200 | bytes 105938944 | tf_op jit(solution)/shard_map/while/body/eval_jaxpr/while/body/eval_jaxpr/qhd,khd->hqk/dot_general | solution.py:213
  1091.1 40.6 %multiply_convert_fusion.6 = bf16[8,512,3072]{2,1,0:T(8,128)(2,1)} fusion(f32[8,512,3072]{2,1,0:T(8,128)} %get-tuple-element.430, f32[8,512,3072]{2,1,0:T(8,128)} %fusion.148, f32[8,512]{1,0:T(8,128)S(1)} %get-tuple-element.431, f32[8,512]{1,0:T(8,128)S(1)} %dynamic-slice_bitcast_fusion.2, pred[512,3072]{1,0:T(8,128)(4,1)S(1)} %broadcast_compare_fusion.5), kind=kLoop, calls=%fused_computation.15.clone.1 | loop fusion | flops 75497472 | bytes 127434752 | tf_op jit(solution)/shard_map/while/body/eval_jaxpr/while/body/eval_jaxpr/convert_element_type | solution.py:217
  1161.7 21.8 dynamic_update_slice.45
  1206.7 24.8 bitcast_add_fusion.5
  1231.6 37.6 %multiply_reduce_fusion.4 = (f32[8,512]{1,0:T(8,128)S(1)}, f32[8,512,3072]{2,1,0:T(8,128)}) fusion(f32[8,512,3072]{2,1,0:T(8,128)} %fusion.148, f32[8,512]{1,0:T(8,128)S(1)} %dynamic-slice_bitcast_fusion.2, pred[512,3072]{1,0:T(8,128)(4,1)S(1)} %broadcast_compare_fusion.5, bf16[3072,8,64]{0,2,1:T(8,128)(2,1)} %get-tuple-element.508, ...), kind=kOutput, calls=%fused_computation.16.clone.1 | convolution fusion | flops 1673523200 | bytes 105938944 | tf_op jit(solution)/shard_map/while/body/eval_jaxpr/while/body/eval_jaxpr/qhd,khd->hqk/dot_general | solution.py:213
  1269.1 40.6 %multiply_convert_fusion.6 = bf16[8,512,3072]{2,1,0:T(8,128)(2,1)} fusion(f32[8,512,3072]{2,1,0:T(8,128)} %get-tuple-element.430, f32[8,512,3072]{2,1,0:T(8,128)} %fusion.148, f32[8,512]{1,0:T(8,128)S(1)} %get-tuple-element.431, f32[8,512]{1,0:T(8,128)S(1)} %dynamic-slice_bitcast_fusion.2, pred[512,3072]{1,0:T(8,128)(4,1)S(1)} %broadcast_compare_fusion.5), kind=kLoop, calls=%fused_computation.15.clone.1 | loop fusion | flops 75497472 | bytes 127434752 | tf_op jit(solution)/shard_map/while/body/eval_jaxpr/while/body/eval_jaxpr/convert_element_type | solution.py:217
  1341.5 21.8 dynamic_update_slice.45
  1386.5 24.8 bitcast_add_fusion.5
  1411.4 37.6 %multiply_reduce_fusion.4 = (f32[8,512]{1,0:T(8,128)S(1)}, f32[8,512,3072]{2,1,0:T(8,128)}) fusion(f32[8,512,3072]{2,1,0:T(8,128)} %fusion.148, f32[8,512]{1,0:T(8,128)S(1)} %dynamic-slice_bitcast_fusion.2, pred[512,3072]{1,0:T(8,128)(4,1)S(1)} %broadcast_compare_fusion.5, bf16[3072,8,64]{0,2,1:T(8,128)(2,1)} %get-tuple-element.508, ...), kind=kOutput, calls=%fused_computation.16.clone.1 | convolution fusion | flops 1673523200 | bytes 105938944 | tf_op jit(solution)/shard_map/while/body/eval_jaxpr/while/body/eval_jaxpr/qhd,khd->hqk/dot_general | solution.py:213
  1448.9 40.6 %multiply_convert_fusion.6 = bf16[8,512,3072]{2,1,0:T(8,128)(2,1)} fusion(f32[8,512,3072]{2,1,0:T(8,128)} %get-tuple-element.430, f32[8,512,3072]{2,1,0:T(8,128)} %fusion.148, f32[8,512]{1,0:T(8,128)S(1)} %get-tuple-element.431, f32[8,512]{1,0:T(8,128)S(1)} %dynamic-slice_bitcast_fusion.2, pred[512,3072]{1,0:T(8,128)(4,1)S(1)} %broadcast_compare_fusion.5), kind=kLoop, calls=%fused_computation.15.clone.1 | loop fusion | flops 75497472 | bytes 127434752 | tf_op jit(solution)/shard_map/while/body/eval_jaxpr/while/body/eval_jaxpr/convert_element_type | solution.py:217
  1521.3 21.8 dynamic_update_slice.45
  1566.3 24.8 bitcast_add_fusion.5
  1591.1 37.6 %multiply_reduce_fusion.4 = (f32[8,512]{1,0:T(8,128)S(1)}, f32[8,512,3072]{2,1,0:T(8,128)}) fusion(f32[8,512,3072]{2,1,0:T(8,128)} %fusion.148, f32[8,512]{1,0:T(8,128)S(1)} %dynamic-slice_bitcast_fusion.2, pred[512,3072]{1,0:T(8,128)(4,1)S(1)} %broadcast_compare_fusion.5, bf16[3072,8,64]{0,2,1:T(8,128)(2,1)} %get-tuple-element.508, ...), kind=kOutput, calls=%fused_computation.16.clone.1 | convolution fusion | flops 1673523200 | bytes 105938944 | tf_op jit(solution)/shard_map/while/body/eval_jaxpr/while/body/eval_jaxpr/qhd,khd->hqk/dot_general | solution.py:213
  1628.7 40.6 %multiply_convert_fusion.6 = bf16[8,512,3072]{2,1,0:T(8,128)(2,1)} fusion(f32[8,512,3072]{2,1,0:T(8,128)} %get-tuple-element.430, f32[8,512,3072]{2,1,0:T(8,128)} %fusion.148, f32[8,512]{1,0:T(8,128)S(1)} %get-tuple-element.431, f32[8,512]{1,0:T(8,128)S(1)} %dynamic-slice_bitcast_fusion.2, pred[512,3072]{1,0:T(8,128)(4,1)S(1)} %broadcast_compare_fusion.5), kind=kLoop, calls=%fused_computation.15.clone.1 | loop fusion | flops 75497472 | bytes 127434752 | tf_op jit(solution)/shard_map/while/body/eval_jaxpr/while/body/eval_jaxpr/convert_element_type | solution.py:217
  1701.1 21.8 dynamic_update_slice.45
  1746.1 24.9 bitcast_add_fusion.5
  1771.0 37.6 %multiply_reduce_fusion.4 = (f32[8,512]{1,0:T(8,128)S(1)}, f32[8,512,3072]{2,1,0:T(8,128)}) fusion(f32[8,512,3072]{2,1,0:T(8,128)} %fusion.148, f32[8,512]{1,0:T(8,128)S(1)} %dynamic-slice_bitcast_fusion.2, pred[512,3072]{1,0:T(8,128)(4,1)S(1)} %broadcast_compare_fusion.5, bf16[3072,8,64]{0,2,1:T(8,128)(2,1)} %get-tuple-element.508, ...), kind=kOutput, calls=%fused_computation.16.clone.1 | convolution fusion | flops 1673523200 | bytes 105938944 | tf_op jit(solution)/shard_map/while/body/eval_jaxpr/while/body/eval_jaxpr/qhd,khd->hqk/dot_general | solution.py:213
  1808.6 40.6 %multiply_convert_fusion.6 = bf16[8,512,3072]{2,1,0:T(8,128)(2,1)} fusion(f32[8,512,3072]{2,1,0:T(8,128)} %get-tuple-element.430, f32[8,512,3072]{2,1,0:T(8,128)} %fusion.148, f32[8,512]{1,0:T(8,128)S(1)} %get-tuple-element.431, f32[8,512]{1,0:T(8,128)S(1)} %dynamic-slice_bitcast_fusion.2, pred[512,3072]{1,0:T(8,128)(4,1)S(1)} %broadcast_compare_fusion.5), kind=kLoop, calls=%fused_computation.15.clone.1 | loop fusion | flops 75497472 | bytes 127434752 | tf_op jit(solution)/shard_map/while/body/eval_jaxpr/while/body/eval_jaxpr/convert_element_type | solution.py:217
  1881.0 21.8 dynamic_update_slice.45
  1926.0 24.8 bitcast_add_fusion.5
  1950.8 37.6 %multiply_reduce_fusion.4 = (f32[8,512]{1,0:T(8,128)S(1)}, f32[8,512,3072]{2,1,0:T(8,128)}) fusion(f32[8,512,3072]{2,1,0:T(8,128)} %fusion.148, f32[8,512]{1,0:T(8,128)S(1)} %dynamic-slice_bitcast_fusion.2, pred[512,3072]{1,0:T(8,128)(4,1)S(1)} %broadcast_compare_fusion.5, bf16[3072,8,64]{0,2,1:T(8,128)(2,1)} %get-tuple-element.508, ...), kind=kOutput, calls=%fused_computation.16.clone.1 | convolution fusion | flops 1673523200 | bytes 105938944 | tf_op jit(solution)/shard_map/while/body/eval_jaxpr/while/body/eval_jaxpr/qhd,khd->hqk/dot_general | solution.py:213
  1988.4 40.6 %multiply_convert_fusion.6 = bf16[8,512,3072]{2,1,0:T(8,128)(2,1)} fusion(f32[8,512,3072]{2,1,0:T(8,128)} %get-tuple-element.430, f32[8,512,3072]{2,1,0:T(8,128)} %fusion.148, f32[8,512]{1,0:T(8,128)S(1)} %get-tuple-element.431, f32[8,512]{1,0:T(8,128)S(1)} %dynamic-slice_bitcast_fusion.2, pred[512,3072]{1,0:T(8,128)(4,1)S(1)} %broadcast_compare_fusion.5), kind=kLoop, calls=%fused_computation.15.clone.1 | loop fusion | flops 75497472 | bytes 127434752 | tf_op jit(solution)/shard_map/while/body/eval_jaxpr/while/body/eval_jaxpr/convert_element_type | solution.py:217
  2060.8 21.8 dynamic_update_slice.45
  2183.1 38.6 %reduce-scatter.10.cloned.1.call-done = bf16[1536,1024]{1,0:T(8,128)(2,1)} async-done(((bf16[3072,1024]{1,0:T(8,128)(2,1)}), bf16[1536,1024]{1,0:T(8,128)(2,1)}) %reduce-scatter.10.cloned.1.call-update) | async-done | bytes 3145744 | tf_op jit(solution)/shard_map/reduce_scatter | solution.py:263
  2268.6 35.1 %convolution_bitcast_fusion = f32[6144,1]{1,0:T(8,128)} fusion(pred[1536,1]{0,1:T(4,128)(4,1)S(1)} %reshape.352, f32[1536,6144]{1,0:T(8,128)} %fusion.46), kind=kOutput, calls=%fused_computation.69 | convolution fusion | flops 113246208 | bytes 37774848
  2311.9 24.4 reduce-scatter.14.cloned.1.call-done
  2336.3 46.2 %reduce-scatter.16.cloned.1.call-done = f32[3072,1]{1,0:T(8,128)} async-done(((f32[6144,1]{1,0:T(8,128)}), f32[3072,1]{1,0:T(8,128)}) %reduce-scatter.16.cloned.1.call-update) | async-done | bytes 12304 | tf_op jit(solution)/shard_map/reshape.47
  2394.9 162.3 %all-reduce.5.cloned.1.call-done = (bf16[1024,3,512]{2,0,1:T(8,128)(2,1)}, bf16[512,1024]{1,0:T(8,128)(2,1)}, bf16[1024,1024]{1,0:T(8,128)(2,1)}, bf16[1024,1024]{1,0:T(8,128)(2,1)}) async-done(((bf16[1024,3,512]{2,0,1:T(8,128)(2,1)}, bf16[512,1024]{1,0:T(8,128)(2,1)}, bf16[1024,1024]{1,0:T(8,128)(2,1)}, bf16[1024,1024]{1,0:T(8,128)(2,1)}), (bf16[1024,3,512]{2,0,1:T(8,128)(2,1)}, ...) | async-done | bytes 8388624 | tf_op jit(solution)/shard_map/psum | solution.py:295
  2572.1 43.8 %all-reduce.1 = (f32[6144]{0:T(1024)S(1)}, f32[3,1024]{1,0:T(4,128)S(1)}, f32[1024]{0:T(1024)}, f32[2048]{0:T(1024)S(1)}, f32[1024]{0:T(1024)}) all-reduce(f32[6144]{0:T(1024)S(1)} %dynamic_update_slice.32, f32[3,1024]{1,0:T(4,128)S(1)} %constant_dynamic-update-slice_fusion.1, ...), channel_id=1, replica_groups=mesh['dp'=16,'head'=2] {'dp','head'}, use_global_device_ids=true, to_apply=%region_20.21 | all-reduce | flops 13312 | bytes 106496 | tf_op jit(solution)/shard_map/psum | solution.py:310
  2630.6 413.8 %all-gather.16.cloned.1.call-done = bf16[16384,3072]{1,0:T(8,128)(2,1)} async-done(((bf16[1024,3072]{1,0:T(8,128)(2,1)}), bf16[16384,3072]{1,0:T(8,128)(2,1)}) %all-gather.16.cloned.1.call-update) | async-done | bytes 100663312 | tf_op jit(solution)/shard_map/all_gather | solution.py:292
  3044.4 34.8 %reduce_sum.169 = bf16[1024,3072]{1,0:T(8,128)(2,1)} reduce(bf16[16,1024,3072]{2,1,0:T(8,128)(2,1)} %bitcast.21, bf16[]{:T(256)} %constant.161.clone.1), dimensions={0}, to_apply=%region_19.20 | reduce | flops 47185920 | bytes 106954752 | tf_op jit(solution)/shard_map/reduce_sum | solution.py:292
  (343 shorter events, 954.9 us)
Async XLA Ops:
  7.2 578.0 %copy-start = (bf16[512,1024]{1,0:T(8,128)(2,1)S(1)}, bf16[512,1024]{1,0:T(8,128)(2,1)}, u32[]{:S(2)}) copy-start(bf16[512,1024]{1,0:T(8,128)(2,1)} %param.25) | copy-start | bytes 3145732
  7.2 115.0 %all-gather.8.cloned.1.call-start = ((), (), s32[]{:S(2)}) async-start(), calls=%async_computation.5 | async-start | bytes 9437184 | tf_op jit(solution)/shard_map/all_gather | solution.py:90
  11.2 21.9 copy-start.23
  14.3 18.8 copy-start.27
  20.6 12.5 copy-start.3
  39.9 696.7 %reduce-scatter.8.cloned.1.call-start = ((), (), s32[]{:S(2)}) async-start(), calls=%async_computation.6 | async-start | bytes 18874368 | tf_op jit(solution)/shard_map/reduce_scatter | solution.py:136
  47.7 116.1 %copy-start.12 = (f32[3072,64]{0,1:T(8,128)}, f32[3072,64]{0,1:T(8,128)S(1)}, u32[]{:S(2)}) copy-start(f32[3072,64]{0,1:T(8,128)S(1)} %get-tuple-element.299) | copy-start | bytes 2359300
  47.7 116.1 %copy-start.15 = (f32[3072,64]{0,1:T(8,128)}, f32[3072,64]{0,1:T(8,128)S(1)}, u32[]{:S(2)}) copy-start(f32[3072,64]{0,1:T(8,128)S(1)} %get-tuple-element.300) | copy-start | bytes 2359300
  163.9 11.9 copy-start.22
  200.2 22.0 copy-start.2
  267.1 22.0 copy-start.2
  334.0 22.0 copy-start.2
  400.9 22.0 copy-start.2
  467.8 22.0 copy-start.2
  534.7 22.0 copy-start.2
  591.9 203.0 %all-gather.10.cloned.1.call-start = ((), (), s32[]{:S(2)}) async-start(), calls=%async_computation.7 | async-start | bytes 6291456 | tf_op jit(solution)/shard_map/all_gather | solution.py:146
  592.6 260.4 %all-gather.12.cloned.1.call-start = ((), (), s32[]{:S(2)}) async-start(), calls=%async_computation.8 | async-start | bytes 6291456 | tf_op jit(solution)/shard_map/all_gather | solution.py:148
  593.2 405.9 %all-gather.14.cloned.1.call-start = ((), (), s32[]{:S(2)}) async-start(), calls=%async_computation.9 | async-start | bytes 9437184 | tf_op jit(solution)/shard_map/all_gather | solution.py:192
  593.2 149.9 %copy-start.39 = (f32[1024]{0:T(1024)}, f32[1024]{0:T(1024)S(1)}, u32[]{:S(2)}) copy-start(f32[1024]{0:T(1024)S(1)} %convert_element_type.169) | copy-start | bytes 12292
  593.3 295.1 %copy-start.43 = (f32[1024]{0:T(1024)}, f32[1024]{0:T(1024)S(1)}, u32[]{:S(2)}) copy-start(f32[1024]{0:T(1024)S(1)} %convert_element_type.173) | copy-start | bytes 12292
  743.2 145.2 %copy-start.25 = (f32[1536]{0:T(1024)}, f32[1536]{0:T(1024)S(1)}, u32[]{:S(2)}) copy-start(f32[1536]{0:T(1024)S(1)} %broadcast_multiply_fusion.4) | copy-start | bytes 18436
  747.6 140.8 %copy-start.31 = (f32[1536]{0:T(1024)}, f32[1536]{0:T(1024)S(1)}, u32[]{:S(2)}) copy-start(f32[1536]{0:T(1024)S(1)} %fusion.67) | copy-start | bytes 18436
  794.9 79.9 %slice-start.2 = ((s8[6291456]{0:T(1024)(128)(4,1)}), s8[2097152]{0:T(1024)(128)(4,1)S(1)}, s32[]{:S(2)}) async-start(s8[6291456]{0:T(1024)(128)(4,1)} %bitcast.142), calls=%async_computation.18 | async-start | bytes 4194304
  853.0 21.8 slice-start.3
  853.0 21.8 copy-start.52
  909.9 8.6 copy-start.33
  918.5 1303.2 %reduce-scatter.10.cloned.1.call-start = ((), (), s32[]{:S(2)}) async-start(), calls=%async_computation.10 | async-start | bytes 9437184 | tf_op jit(solution)/shard_map/reduce_scatter | solution.py:263
  2092.3 9.4 copy-start.16
  2144.4 167.5 %reduce-scatter.12.cloned.1.call-start = ((), (), s32[]{:S(2)}) async-start(), calls=%async_computation.11 | async-start | bytes 6291456 | tf_op jit(solution)/shard_map/reduce_scatter | solution.py:177
  2155.8 180.4 %reduce-scatter.14.cloned.1.call-start = ((), (), s32[]{:S(2)}) async-start(), calls=%async_computation.12 | async-start | bytes 6291456 | tf_op jit(solution)/shard_map/reduce_scatter | solution.py:183
  2167.1 215.4 %reduce-scatter.16.cloned.1.call-start = ((), (), s32[]{:S(2)}) async-start(), calls=%async_computation.14 | async-start | bytes 4718592 | tf_op jit(solution)/shard_map/reshape.47
  2167.2 54.5 %copy-start.24 = (f32[1536]{0:T(1024)S(1)}, f32[1536]{0:T(1024)}, u32[]{:S(2)}) copy-start(f32[1536]{0:T(1024)} %copy-done.23) | copy-start | bytes 18436
  2183.1 45.2 %copy-start.30 = (f32[1536]{0:T(1024)S(1)}, f32[1536]{0:T(1024)}, u32[]{:S(2)}) copy-start(f32[1536]{0:T(1024)} %copy-done.29) | copy-start | bytes 18436
  2232.1 9.6 copy-start.7
  2232.1 9.6 copy-start.34
  2232.1 9.6 copy-start.40
  2232.1 22.5 slice-start.8
  2232.1 25.9 slice-start.4
  2241.7 12.9 slice-start.9
  2241.7 16.3 slice-start.5
  2303.7 253.5 %all-reduce.5.cloned.1.call-start = ((), (), s32[]{:S(2)}) async-start(), calls=%async_computation.15 | async-start | bytes 16777216 | tf_op jit(solution)/shard_map/psum | solution.py:295
  2311.9 24.4 copy-start.45
  2336.3 708.1 %all-gather.16.cloned.1.call-start = ((), (), s32[]{:S(2)}) async-start(), calls=%async_computation.13 | async-start | bytes 106954752 | tf_op jit(solution)/shard_map/all_gather | solution.py:292
  2560.2 8.7 copy-start.20
  2565.8 51.4 %copy-start.17 = (f32[3072,1]{1,0:T(8,128)S(1)}, f32[3072,1]{1,0:T(8,128)}, u32[]{:S(2)}) copy-start(f32[3072,1]{1,0:T(8,128)} %reduce-scatter.16.cloned.1.call-done) | copy-start | bytes 36868
  2568.8 61.2 %copy-start.36 = (bf16[1,1024]{1,0:T(2,128)(2,1)S(1)}, bf16[1,1024]{1,0:T(2,128)(2,1)}, u32[]{:S(2)}) copy-start(bf16[1,1024]{1,0:T(2,128)(2,1)} %param.19) | copy-start | bytes 6148
  2568.8 61.2 %copy-start.38 = (f32[1,1024]{1,0:T(1,128)S(1)}, f32[1,1024]{1,0:T(1,128)}, u32[]{:S(2)}) copy-start(f32[1,1024]{1,0:T(1,128)} %copy-done.37) | copy-start | bytes 12292
  3044.4 44.0 %copy-start.1 = (bf16[512,1024]{1,0:T(8,128)(2,1)S(1)}, bf16[512,1024]{1,0:T(8,128)(2,1)}, u32[]{:S(2)}) copy-start(bf16[512,1024]{1,0:T(8,128)(2,1)} %param.25) | copy-start | bytes 3145732
  (32 other events, 141.9 us)
Sparse Core Ops, SparseCore 0:
  40.0 82.1 all-gather.7
  592.0 144.5 reduce-scatter.7
  738.1 56.7 all-gather.9
  796.3 56.7 all-gather.11
  918.7 80.3 all-gather.13
  2144.5 77.1 reduce-scatter.9
  2224.6 54.3 reduce-scatter.11
  2281.8 54.3 reduce-scatter.13
  2339.1 43.4 reduce-scatter.15
  2387.0 170.1 all-reduce.4
  2559.4 484.9 all-gather.15
